TPU v7x, 32 devices: a whole 2x2x4 slice. The times are simulated.
32 devices in a mesh: grp: 2 (over x), row: 2 (over core), col: 8 (over z, y).
Axes of the slice: x: 2, y: 2, z: 4, core: 2. Of those that a mesh axis runs over, the one named last changes fastest.
Arguments:
- hidden_acts: bfloat16 [512, 26624], P(('grp', 'row'), 'col'), parts along dimension 0, may hold values from -216 to 216
- down_weight: bfloat16 [26624, 8192], P('col', 'row'), may hold values from -0.0390625 to 0.0390625
- amax_history: float32 [8], P('grp'), parts along dimension 0, may hold values from 3 to 12
Outputs:
- scaled_out: bfloat16 [512, 8192], P(('grp', 'col'), 'row'), parts along dimension 0
- token_scale: float32 [512], P(('grp', 'row')), parts along dimension 0
- history_next: float32 [8], P('grp'), parts along dimension 0
There are 2 independent parts, one for each index of `grp`. A program takes and returns all parts, laid end to end along the dimension named above; an argument that names none is the same for every part. Nothing has to cross between parts.
All inputs are finite; a program needn't handle non-finite values.
Results may differ from a plain program's by a relative error of at most 0.0044.
Values may be sent and summed in bfloat16 or wider, within the bound.
No kernel may reach another device: no remote copies, remote signals or barrier semaphores. Data moves between devices by JAX's collectives and lax.ppermute only.
A program may use at most 64 MiB of HBM per device.

v0:
```python
import jax
import jax.numpy as jnp
from jax import lax
from jax.sharding import PartitionSpec as P

clip_ratio = 0.5
format_limit = 448.0


def clip_scaled(values, scales):
    return jnp.clip(
        values.astype(jnp.float32) / scales[:, None], -format_limit, format_limit
    ).astype(jnp.bfloat16)


def on_device(hidden_acts, down_weight, amax_history):
    local_peak = jnp.max(jnp.abs(hidden_acts), axis=1).astype(jnp.float32)
    token_peak = lax.pmax(local_peak, "col")
    own_scale = clip_ratio * (token_peak + 1e-06) / format_limit
    quantized = clip_scaled(hidden_acts, own_scale)
    all_quant = lax.all_gather(quantized, "row", axis=0, tiled=True)
    all_scale = lax.all_gather(own_scale, "row", axis=0, tiled=True)
    previous = jnp.max(amax_history)
    block_rows = all_quant.shape[0] // lax.axis_size("col")
    summed = lax.psum_scatter(
        jnp.dot(all_quant, down_weight, preferred_element_type=jnp.float32),
        "col",
        scatter_dimension=0,
        tiled=True,
    )
    block_scale = lax.dynamic_slice_in_dim(
        all_scale, lax.axis_index("col") * block_rows, block_rows
    )
    result = summed * block_scale[:, None]
    local_max = jnp.max(jnp.abs(result))
    scaled_out = jnp.clip(result / previous, -1.0, 1.0).astype(jnp.bfloat16)
    newest = lax.pmax(local_max, ("row", "col"))
    history_next = jnp.concatenate([newest[None], amax_history[:-1]])
    return (scaled_out, own_scale, history_next)


def solution(mesh):
    in_specs = (P(("grp", "row"), "col"), P("col", "row"), P("grp"))
    out_specs = (P(("grp", "col"), "row"), P(("grp", "row")), P("grp"))
    return jax.shard_map(
        on_device, mesh=mesh, in_specs=in_specs, out_specs=out_specs, check_vma=False
    )
```

profile of v0, /device:TPU:0, one launch (start us, length us, event | category | flops | bytes accessed | tf_op | source)
XLA Modules:
  0.0 189.5 jit_solution(5066335631180745152)
XLA Ops:
  7.2 0.0 all-gather.3.cloned.1.call-start
  7.2 1.4 abs_reduce_fusion
  8.6 23.2 %pmax.14 = f32[128]{0:T(128)S(1)} all-reduce(bf16[128]{0:T(256)(128)(2,1)S(1)} %abs_reduce_fusion), channel_id=1, replica_groups=mesh['grp'=2,'row'=2,'col'=8] {'col'}, use_global_device_ids=true, to_apply=%region_1.0 | all-reduce | flops 128 | bytes 768 | tf_op jit(solution)/shard_map/pmax | solution.py:18
  31.8 0.0 copy-start
  31.8 2.3 %clamp_convert_fusion = bf16[128,3328]{1,0:T(8,128)(2,1)} fusion(bf16[128,3328]{1,0:T(8,128)(2,1)} %param.3, f32[128]{0:T(128)S(1)} %add_multiply_fusion), kind=kLoop, calls=%fused_computation | loop fusion | flops 1703936 | bytes 1704448 | tf_op jit(solution)/shard_map/convert_element_type | solution.py:13
  34.1 0.0 all-gather.3.cloned.1.call-update
  34.1 0.0 reduce-scatter.2.cloned.1.call-start
  34.2 7.4 %all-gather.3.cloned.1.call-done = bf16[256,3328]{1,0:T(8,128)(2,1)} async-done(((bf16[128,3328]{1,0:T(8,128)(2,1)}), bf16[256,3328]{1,0:T(8,128)(2,1)}) %all-gather.3.cloned.1.call-update) | async-done | bytes 1703952 | tf_op jit(solution)/shard_map/all_gather | solution.py:21
  41.5 14.3 %fusion = f32[256,4096]{1,0:T(8,128)} fusion(bf16[256,3328]{1,0:T(8,128)(2,1)} %all-gather.3.cloned.1.call-done, bf16[3328,4096]{1,0:T(8,128)(2,1)} %param.4), kind=kOutput, calls=%fused_computation.6 | convolution fusion | flops 6979321856 | bytes 33161216 | tf_op jit(solution)/shard_map/dot_general | solution.py:26
  55.8 0.0 copy-done
  55.8 0.0 copy-start.1
  55.8 0.0 reduce-scatter.2.cloned.1.call-update
  55.9 1.8 all-gather
  57.7 0.1 dynamic_slice.3
  57.7 0.0 copy-done.1
  57.7 0.6 reduce_max.28
  58.3 87.1 %reduce-scatter.2.cloned.1.call-done = f32[32,4096]{1,0:T(8,128)} async-done(((f32[256,4096]{1,0:T(8,128)}), f32[32,4096]{1,0:T(8,128)}) %reduce-scatter.2.cloned.1.call-update) | async-done | bytes 524304 | tf_op jit(solution)/shard_map/reduce_scatter | solution.py:25
  145.5 3.2 %abs_reduce_fusion.1 = (f32[]{:T(128)}, bf16[32,4096]{1,0:T(8,128)(2,1)}) fusion(f32[32,4096]{1,0:T(8,128)} %reduce-scatter.2.cloned.1.call-done, f32[32]{0:T(128)S(1)} %dynamic_slice.3, f32[]{:T(128)} %reduce_max.28), kind=kLoop, calls=%fused_computation.2 | loop fusion | flops 786431 | bytes 786568 | tf_op jit(solution)/shard_map/reduce_max | solution.py:35
  148.7 32.8 %pmax.15 = f32[1]{0:T(128)} all-reduce(f32[1]{0:T(128)} %bitcast.2), channel_id=1, replica_groups=mesh['grp'=2,'row'=2,'col'=8] {'row','col'}, use_global_device_ids=true, to_apply=%region_5.6 | all-reduce | flops 1 | bytes 8 | tf_op jit(solution)/shard_map/pmax | solution.py:37
  181.5 1.1 pad_maximum_fusion
  (2 shorter events, 0.0 us)
Async XLA Ops:
  7.2 34.4 %all-gather.3.cloned.1.call-start = ((), (), s32[]{:S(2)}) async-start(), calls=%async_computation.1 | async-start | bytes 2555904 | tf_op jit(solution)/shard_map/all_gather | solution.py:21
  31.8 24.0 %copy-start = (f32[128]{0:T(128)}, f32[128]{0:T(128)S(1)}, u32[]{:S(2)}) copy-start(f32[128]{0:T(128)S(1)} %add_multiply_fusion) | copy-start | bytes 1540
  34.1 111.3 %reduce-scatter.2.cloned.1.call-start = ((), (), s32[]{:S(2)}) async-start(), calls=%async_computation.2 | async-start | bytes 4718592 | tf_op jit(solution)/shard_map/reduce_scatter | solution.py:25
  55.8 1.9 %copy-start.1 = (f32[4]{0:T(128)S(1)}, f32[4]{0:T(128)}, u32[]{:S(2)}) copy-start(f32[4]{0:T(128)} %param.5) | copy-start | bytes 52
Sparse Core Ops, SparseCore 0:
  34.2 7.2 all-gather.2
  56.0 89.4 reduce-scatter.1
where the time goes:
time: 190 us; the launch traced here: 189 us
  waiting for transfers between devices  94.5 us (50%)
  blocking collectives  57.8 us (30%)
  matrix products  14.3 us (8%)
  between operations  14.1 us (7%)
  other arithmetic  8.67 us (5%)
    reduce_scatter x1, waiting for transfers between devices, on_device(): lax.psum_scatter(jnp.dot(all_quant, down_weight, preferred_element_type=j...  87.1 us
    pmax x1, blocking collectives, on_device(): newest = lax.pmax(local_max, ('row', 'col'))  32.8 us
    pmax x1, blocking collectives, on_device(): token_peak = lax.pmax(local_peak, 'col')  23.2 us
    dot_general x1, matrix products, on_device(): jnp.dot(all_quant, down_weight, preferred_element_type=jnp.float32)  14.3 us
    all_gather x1, waiting for transfers between devices, on_device(): all_quant = lax.all_gather(quantized, 'row', axis=0, tiled=True)  7.35 us
  transfers between devices with their start and end apart: 2, of which 2 were waited for; matrix products, arithmetic and copies ran while one was open for 0% of the time, Pallas kernels for 0%

commit v1 on v0

--- a/solution.py
+++ b/solution.py
@@ -18,7 +18,9 @@
     token_peak = lax.pmax(local_peak, "col")
     own_scale = clip_ratio * (token_peak + 1e-06) / format_limit
     quantized = clip_scaled(hidden_acts, own_scale)
-    all_quant = lax.all_gather(quantized, "row", axis=0, tiled=True)
+    all_quant = jnp.concatenate(
+        lax.all_to_all(jnp.stack([quantized] * lax.axis_size("row")), "row", 0, 0), axis=0
+    )
     all_scale = lax.all_gather(own_scale, "row", axis=0, tiled=True)
     previous = jnp.max(amax_history)
     block_rows = all_quant.shape[0] // lax.axis_size("col")

time: 190 us -> 184 us (0.968)
  waiting for transfers between devices: 94.5 us -> 83.2 us
  blocking collectives: 57.8 us -> 62.9 us
    all_gather x1 -> x0, waiting for transfers between devices: 7.35 us -> none  [on_device(): all_quant = lax.all_gather(quantized, 'row', axis=0, tiled=True)]
    all_to_all x0 -> x1, blocking collectives: none -> 5.1 us  [on_device(): lax.all_to_all(jnp.stack([quantized] * lax.axis_size('row')), 'row', 0, 0)]
    reduce_scatter x1, waiting for transfers between devices: 87.1 us -> 83.2 us  [on_device(): lax.psum_scatter(jnp.dot(all_quant, down_weight, preferred_element_type=j...]
    convert_element_type x1 -> x0, other arithmetic: 2.33 us -> none  [clip_scaled(): return jnp.clip(values.astype(jnp.float32) / scales[:, None], -format_lim...]
  transfers between devices with their start and end apart: 2 -> 1, of which waited for: 2 -> 1; matrix products, arithmetic and copies ran while one was open for 0% -> 0% of each run, Pallas kernels for 0% -> 0%
where the time goes in v1:
time: 184 us; the launch traced here: 183 us
  waiting for transfers between devices  83.2 us (45%)
  blocking collectives  62.9 us (34%)
  matrix products  15.2 us (8%)
  between operations  14.1 us (8%)
  other arithmetic  7.91 us (4%)
    reduce_scatter x1, waiting for transfers between devices, on_device(): lax.psum_scatter(jnp.dot(all_quant, down_weight, preferred_element_type=j...  83.2 us
    pmax x1, blocking collectives, on_device(): newest = lax.pmax(local_max, ('row', 'col'))  32.8 us
    pmax x1, blocking collectives, on_device(): token_peak = lax.pmax(local_peak, 'col')  23.2 us
    dot_general x1, matrix products, on_device(): jnp.dot(all_quant, down_weight, preferred_element_type=jnp.float32)  15.2 us
    all_to_all x1, blocking collectives, on_device(): lax.all_to_all(jnp.stack([quantized] * lax.axis_size('row')), 'row', 0, 0)  5.1 us
  transfers between devices with their start and end apart: 1, of which 1 were waited for; matrix products, arithmetic and copies ran while one was open for 0% of the time, Pallas kernels for 0%

profile of v1, /device:TPU:0, one launch (start us, length us, event | category | flops | bytes accessed | tf_op | source)
XLA Modules:
  0.0 183.4 jit_solution(12844243246227661822)
XLA Ops:
  7.2 0.0 reduce-scatter.2.cloned.1.call-start
  7.2 1.4 abs_reduce_fusion
  8.6 23.2 %pmax.14 = f32[128]{0:T(128)S(1)} all-reduce(bf16[128]{0:T(256)(128)(2,1)S(1)} %abs_reduce_fusion), channel_id=1, replica_groups=mesh['grp'=2,'row'=2,'col'=8] {'col'}, use_global_device_ids=true, to_apply=%region_1.0 | all-reduce | flops 128 | bytes 768 | tf_op jit(solution)/shard_map/pmax | solution.py:18
  31.8 0.0 copy-start
  31.8 1.4 fusion
  33.2 0.1 pad_maximum_fusion
  33.4 0.0 copy-done
  33.4 5.1 %all_to_all.5 = bf16[2,128,3328]{2,1,0:T(8,128)(2,1)S(1)} all-to-all(bf16[2,128,3328]{2,1,0:T(8,128)(2,1)S(1)} %pad_maximum_fusion), channel_id=1, replica_groups=mesh['grp'=2,'row'=2,'col'=8] {'row'}, dimensions={0} | all-to-all | bytes 3407872 | tf_op jit(solution)/shard_map/all_to_all | solution.py:22
  38.5 15.2 %fusion.1 = f32[256,4096]{1,0:T(8,128)} fusion(bf16[256,3328]{1,0:T(8,128)(2,1)S(1)} %bitcast.10, bf16[3328,4096]{1,0:T(8,128)(2,1)} %param.4), kind=kOutput, calls=%fused_computation.8 | convolution fusion | flops 6979321856 | bytes 33161216 | tf_op jit(solution)/shard_map/dot_general | solution.py:28
  53.7 0.0 copy-start.1
  53.7 0.0 reduce-scatter.2.cloned.1.call-update
  53.7 1.8 all-gather
  55.5 0.1 dynamic_slice.3
  55.6 0.0 copy-done.1
  55.6 0.6 reduce_max.28
  56.2 83.2 %reduce-scatter.2.cloned.1.call-done = f32[32,4096]{1,0:T(8,128)} async-done(((f32[256,4096]{1,0:T(8,128)}), f32[32,4096]{1,0:T(8,128)}) %reduce-scatter.2.cloned.1.call-update) | async-done | bytes 524304 | tf_op jit(solution)/shard_map/reduce_scatter | solution.py:27
  139.4 3.2 %abs_reduce_fusion.1 = (f32[]{:T(128)}, bf16[32,4096]{1,0:T(8,128)(2,1)}) fusion(f32[32,4096]{1,0:T(8,128)} %reduce-scatter.2.cloned.1.call-done, f32[32]{0:T(128)S(1)} %dynamic_slice.3, f32[]{:T(128)} %reduce_max.28), kind=kLoop, calls=%fused_computation.4 | loop fusion | flops 786431 | bytes 786568 | tf_op jit(solution)/shard_map/reduce_max | solution.py:37
  142.6 32.8 %pmax.15 = f32[1]{0:T(128)} all-reduce(f32[1]{0:T(128)} %bitcast.4), channel_id=1, replica_groups=mesh['grp'=2,'row'=2,'col'=8] {'row','col'}, use_global_device_ids=true, to_apply=%region_5.6 | all-reduce | flops 1 | bytes 8 | tf_op jit(solution)/shard_map/pmax | solution.py:39
  175.4 1.1 pad_maximum_fusion.1
  (2 shorter events, 0.0 us)
Async XLA Ops:
  7.2 132.2 %reduce-scatter.2.cloned.1.call-start = ((), (), s32[]{:S(2)}) async-start(), calls=%async_computation.2 | async-start | bytes 4718592 | tf_op jit(solution)/shard_map/reduce_scatter | solution.py:27
  31.8 1.6 copy-start
  53.7 1.9 %copy-start.1 = (f32[4]{0:T(128)S(1)}, f32[4]{0:T(128)}, u32[]{:S(2)}) copy-start(f32[4]{0:T(128)} %param.5) | copy-start | bytes 52
Sparse Core Ops, SparseCore 0:
  53.8 85.5 reduce-scatter.1
